TPU v7x, 512 devices: a whole 4x4x16 slice. The times are simulated.
512 devices in a mesh: gx: 64 (over y, z), ta: 8 (over x, core).
Axes of the slice: x: 4, y: 4, z: 16, core: 2. Of those that a mesh axis runs over, the one named last changes fastest.
Arguments:
- query_vecs: bfloat16 [256, 64, 5120], P('gx', None, 'ta'), may hold values from -32 to 32
- key_vecs: bfloat16 [256, 64, 5120], P('gx', None, 'ta'), may hold values from -6 to 6
- value_vecs: bfloat16 [256, 64, 5120], P('gx', None, 'ta'), may hold values from -6 to 6
- slot_map: int32 [16, 64], replicated, may hold values from 0 to 63, each once within a row
- edge_list: int32 [256, 2], replicated, may hold values from 0 to 63
- edge_types: int32 [256], replicated, may hold values from 0 to 2
- type_gain: float32 [2, 3, 5120], P(None, None, 'ta'), may hold values from 0.25 to 2
- norm_gain: float32 [2, 5120], P(None, 'ta'), may hold values from 0.5 to 2
- gate_proj: bfloat16 [2, 5120, 20480], P(None, 'ta', 'gx'), may hold values from -0.078125 to 0.078125
- up_proj: bfloat16 [2, 5120, 20480], P(None, 'ta', 'gx'), may hold values from -0.078125 to 0.078125
- down_proj: bfloat16 [2, 20480, 5120], P(None, 'gx', 'ta'), may hold values from -0.0390625 to 0.0390625
Outputs:
- node_states: bfloat16 [512, 5120], P('gx', 'ta')
All inputs are finite; a program needn't handle non-finite values.
Results may differ from a plain program's by a relative error of at most 0.04.
Values may be sent and summed in bfloat16 or wider, within the bound.
A program may use at most 64 MiB of HBM per device.

v0:
```python
import jax
import jax.numpy as jnp
from jax import lax
from jax.sharding import PartitionSpec as P

D = 5120
HEAD_DIM = 128
VENUES = 16
STEPS = 16
NODE_STEPS = 8
ROUNDS = 2
ETYPES = 3


def settle_rows(nodes, hidden, down_local, row_begin, rows_dev):
    summed = lax.psum_scatter(
        jnp.dot(hidden, down_local, preferred_element_type=jnp.float32),
        "gx",
        scatter_dimension=0,
        tiled=True,
    )
    base_rows = lax.dynamic_slice_in_dim(nodes, row_begin, rows_dev, 0)
    return (base_rows.astype(jnp.float32) + summed).astype(jnp.bfloat16)


def per_device(
    query_vecs,
    key_vecs,
    value_vecs,
    slot_map,
    edge_list,
    edge_types,
    type_gain,
    norm_gain,
    gate_proj,
    up_proj,
    down_proj,
):
    pairs_dev = query_vecs.shape[0]
    inst_total = query_vecs.shape[1]
    feat_width = query_vecs.shape[2]
    head_count = feat_width // HEAD_DIM
    gx_count = lax.axis_size("gx")
    inst_local = inst_total // gx_count
    score_scale = 1.0 / HEAD_DIM**0.5
    venue_idx = lax.axis_index("gx") * pairs_dev // STEPS
    slot_order = lax.dynamic_index_in_dim(slot_map, venue_idx, 0, keepdims=False)
    split_shape = (pairs_dev, gx_count, inst_local, feat_width)
    sorted_queries = jnp.take(query_vecs, slot_order, axis=1).reshape(split_shape)
    sorted_keys = jnp.take(key_vecs, slot_order, axis=1).reshape(split_shape)
    sorted_values = jnp.take(value_vecs, slot_order, axis=1).reshape(split_shape)
    query_steps = jnp.arange(VENUES * NODE_STEPS) % NODE_STEPS + (STEPS - NODE_STEPS)
    key_steps = jnp.arange(VENUES * STEPS) % STEPS
    allowed = key_steps[None, :] <= query_steps[:, None]
    queries = lax.all_to_all(sorted_queries, "gx", split_axis=1, concat_axis=0, tiled=True)
    keyset = lax.all_to_all(sorted_keys, "gx", split_axis=1, concat_axis=0, tiled=True)
    valueset = lax.all_to_all(sorted_values, "gx", split_axis=1, concat_axis=0, tiled=True)
    pair_total = queries.shape[0]
    item_count = queries.shape[2]
    queries = queries.reshape(VENUES, STEPS, item_count, head_count, HEAD_DIM)[
        :, STEPS - NODE_STEPS :
    ]
    queries = queries.reshape(VENUES * NODE_STEPS, item_count, head_count, HEAD_DIM)
    keyset = keyset.reshape(pair_total, item_count, head_count, HEAD_DIM)
    valueset = valueset.reshape(pair_total, item_count, head_count, HEAD_DIM)
    scores = (
        jnp.einsum("qnhd,knhd->nhqk", queries, keyset, preferred_element_type=jnp.float32)
        * score_scale
    )
    scores = jnp.where(allowed[None, None], scores, jnp.float32(-1e30))
    row_max = jnp.max(scores, axis=-1, keepdims=True)
    expd = jnp.exp(scores - row_max)
    probs = (expd / jnp.sum(expd, axis=-1, keepdims=True)).astype(jnp.bfloat16)
    attended = jnp.einsum("nhqk,knhd->nqhd", probs, valueset, preferred_element_type=jnp.float32)
    attended = attended.reshape(item_count, VENUES, NODE_STEPS, feat_width)
    pooled = jnp.mean(attended, axis=1).astype(jnp.bfloat16)
    own_rows = pooled.reshape(inst_local * NODE_STEPS, feat_width)
    rows_dev = own_rows.shape[0]
    row_begin = lax.axis_index("gx") * rows_dev
    nodes = lax.all_gather(own_rows, "gx", axis=0, tiled=True)
    row_total = nodes.shape[0]
    node_ids = jnp.arange(inst_total)
    type_ids = jnp.arange(ETYPES)
    at_source = (edge_list[:, 0][:, None] == node_ids[None, :]).astype(jnp.float32)
    at_target = (edge_list[:, 1][:, None] == node_ids[None, :]).astype(jnp.float32)
    of_type = (edge_types[:, None] == type_ids[None, :]).astype(jnp.float32)
    adjacency = jnp.einsum("et,ei,ej->tij", of_type, at_target, at_source)
    degree = jnp.maximum(jnp.sum(at_target, axis=0), 1.0)
    adj_rows = adjacency.reshape(ETYPES * inst_total, inst_total).astype(jnp.bfloat16)
    for layer_idx in range(ROUNDS):
        flat_nodes = nodes.reshape(inst_total, NODE_STEPS * feat_width)
        gathered = jnp.dot(adj_rows, flat_nodes, preferred_element_type=jnp.float32)
        gathered = gathered.reshape(ETYPES, inst_total, NODE_STEPS, feat_width)
        message = (
            jnp.sum(gathered * type_gain[layer_idx][:, None, None, :], axis=0)
            / degree[:, None, None]
        )
        pre_norm = nodes.astype(jnp.float32) + message.reshape(row_total, feat_width)
        squares = lax.psum(jnp.sum(pre_norm * pre_norm, axis=-1), "ta")
        row_scale = lax.rsqrt(squares / D + 1e-05)[:, None]
        normed = (pre_norm * row_scale * norm_gain[layer_idx][None, :]).astype(jnp.bfloat16)
        gate_part = jnp.dot(normed, gate_proj[layer_idx], preferred_element_type=jnp.float32)
        up_part = jnp.dot(normed, up_proj[layer_idx], preferred_element_type=jnp.float32)
        gate_sum, up_sum = (
            lax.psum(gate_part.astype(jnp.bfloat16), "ta").astype(jnp.float32),
            lax.psum(up_part.astype(jnp.bfloat16), "ta").astype(jnp.float32),
        )
        hidden = (jax.nn.silu(gate_sum) * up_sum).astype(jnp.bfloat16)
        down_local = down_proj[layer_idx]
        if layer_idx == ROUNDS - 1:
            own_rows = settle_rows(nodes, hidden, down_local, row_begin, rows_dev)
        else:
            own_rows = settle_rows(nodes, hidden, down_local, row_begin, rows_dev)
            nodes = lax.all_gather(own_rows, "gx", axis=0, tiled=True)
    return own_rows


def solution(mesh):
    placed = (
        P("gx", None, "ta"),
        P("gx", None, "ta"),
        P("gx", None, "ta"),
        P(),
        P(),
        P(),
        P(None, None, "ta"),
        P(None, "ta"),
        P(None, "ta", "gx"),
        P(None, "ta", "gx"),
        P(None, "gx", "ta"),
    )
    return jax.shard_map(
        per_device, mesh=mesh, in_specs=placed, out_specs=P("gx", "ta"), check_vma=False
    )
```

profile of v0, /device:TPU:2, one launch (start us, length us, event | category | flops | bytes accessed | tf_op | source)
XLA Modules:
  0.0 1049.3 jit_solution(5708310502350677954)
XLA Ops:
  6.5 0.7 compare_and_fusion
  7.3 0.2 copy-done
  7.5 1.6 gather_fusion
  9.1 1.6 gather_fusion.1
  10.8 1.6 gather_fusion.2
  12.4 0.2 select_bitcast_fusion.1
  12.5 1.0 copy.32
  13.5 18.9 %all-to-all-start.1 = ((bf16[4,64,1,640]{3,0,2,1:T(4,128)(2,1)}), bf16[4,64,1,640]{3,0,2,1:T(4,128)(2,1)S(1)}, u32[]{:S(2)}, u32[]{:S(2)}) async-start(bf16[4,64,1,640]{3,0,2,1:T(4,128)(2,1)} %copy.32), calls=%async_computation.1 | async-start | bytes 655360 | tf_op jit(solution)/shard_map/all_to_all | solution.py:55
  32.4 1.0 copy.34
  33.4 22.7 %all-to-all-done.1 = bf16[4,64,1,640]{3,0,2,1:T(4,128)(2,1)S(1)} async-done(((bf16[4,64,1,640]{3,0,2,1:T(4,128)(2,1)}), bf16[4,64,1,640]{3,0,2,1:T(4,128)(2,1)S(1)}, u32[]{:S(2)}, u32[]{:S(2)}) %all-to-all-start.1) | async-done | bytes 327712 | tf_op jit(solution)/shard_map/all_to_all | solution.py:55
  56.1 6.5 all-to-all-start.2
  62.6 1.0 copy.31
  63.6 0.1 fusion.49
  63.8 0.1 div.64
  64.0 21.6 %all-to-all-done.2 = bf16[4,64,1,640]{3,0,2,1:T(4,128)(2,1)S(1)} async-done(((bf16[4,64,1,640]{3,0,2,1:T(4,128)(2,1)}), bf16[4,64,1,640]{3,0,2,1:T(4,128)(2,1)S(1)}, u32[]{:S(2)}, u32[]{:S(2)}) %all-to-all-start.2) | async-done | bytes 327712 | tf_op jit(solution)/shard_map/all_to_all | solution.py:56
  85.6 6.6 all-to-all-start
  92.2 0.2 fusion.6
  92.5 0.1 reshape.143
  92.7 0.1 reshape.146
  92.9 0.5 fusion.68
  93.3 0.3 fusion.5
  93.6 20.9 %all-to-all-done = bf16[4,64,1,640]{3,0,2,1:T(4,128)(2,1)S(1)} async-done(((bf16[4,64,1,640]{3,0,2,1:T(4,128)(2,1)}), bf16[4,64,1,640]{3,0,2,1:T(4,128)(2,1)S(1)}, u32[]{:S(2)}, u32[]{:S(2)}) %all-to-all-start) | async-done | bytes 327712 | tf_op jit(solution)/shard_map/all_to_all | solution.py:57
  114.5 0.1 reshape.141
  114.6 1.4 convolution_bitcast_fusion
  116.0 0.2 copy.37
  116.4 99.8 %all_gather.6 = bf16[512,640]{1,0:T(8,128)(2,1)S(1)} all-gather(bf16[8,640]{1,0:T(8,128)(2,1)S(1)} %multiply_convert_fusion.2), channel_id=1, replica_groups=mesh['gx'=64,'ta'=8] {'gx'}, dimensions={0}, use_global_device_ids=true | all-gather | bytes 665600 | tf_op jit(solution)/shard_map/all_gather | solution.py:80
  216.2 0.3 reshape.148
  216.5 0.7 multiply_reduce_fusion.1
  217.2 0.9 multiply_reduce_fusion.3
  218.1 10.0 psum.42
  228.1 1.3 convolution_convert_fusion.3
  229.4 1.3 convolution_convert_fusion.2
  230.7 67.0 %all-reduce.15.cloned.1.call-done = (bf16[512,320]{0,1:T(8,128)(2,1)}, bf16[512,320]{0,1:T(8,128)(2,1)}) async-done(((bf16[512,320]{0,1:T(8,128)(2,1)}, bf16[512,320]{0,1:T(8,128)(2,1)}), (bf16[512,320]{0,1:T(8,128)(2,1)}, bf16[512,320]{0,1:T(8,128)(2,1)})) %all-reduce.15.cloned.1.call-update) | async-done | bytes 655376 | tf_op jit(solution)/shard_map/psum | solution.py:106
  297.7 2.9 fusion.23
  300.7 1.3 dynamic-slice
  302.6 275.2 %all-reduce.9.cloned.1.call-done = f32[512,640]{1,0:T(8,128)} async-done(((f32[512,640]{1,0:T(8,128)}), f32[512,640]{1,0:T(8,128)}) %all-reduce.9.cloned.1.call-update) | async-done | bytes 1310736
  577.8 0.7 fusion.51
  578.6 98.7 %all_gather.7 = bf16[512,640]{1,0:T(8,128)(2,1)S(1)} all-gather(bf16[8,640]{1,0:T(8,128)(2,1)S(1)} %fusion.51), channel_id=1, replica_groups=mesh['gx'=64,'ta'=8] {'gx'}, dimensions={0}, use_global_device_ids=true | all-gather | bytes 665600 | tf_op jit(solution)/shard_map/all_gather | solution.py:114
  677.3 0.3 reshape.149
  677.6 0.7 multiply_reduce_fusion
  678.3 0.9 multiply_reduce_fusion.2
  679.2 10.0 psum.45
  689.2 1.3 convolution_convert_fusion.1
  690.5 1.2 convolution_convert_fusion
  691.8 69.7 %all-reduce.13.cloned.1.call-done = (bf16[512,320]{0,1:T(8,128)(2,1)}, bf16[512,320]{0,1:T(8,128)(2,1)}) async-done(((bf16[512,320]{0,1:T(8,128)(2,1)}, bf16[512,320]{0,1:T(8,128)(2,1)}), (bf16[512,320]{0,1:T(8,128)(2,1)}, bf16[512,320]{0,1:T(8,128)(2,1)})) %all-reduce.13.cloned.1.call-update) | async-done | bytes 655376 | tf_op jit(solution)/shard_map/psum | solution.py:106
  761.5 2.8 fusion.19
  764.3 277.2 %all-reduce.11.cloned.1.call-done = f32[512,640]{1,0:T(8,128)} async-done(((f32[512,640]{1,0:T(8,128)}), f32[512,640]{1,0:T(8,128)}) %all-reduce.11.cloned.1.call-update) | async-done | bytes 1310736
  1041.4 1.3 fusion.50
  (48 shorter events, 0.7 us)
Async XLA Ops:
  6.5 1.0 copy-start
  7.5 1.6 copy-start.1
  9.1 1.6 copy-start.2
  13.5 50.0 %copy-start.6 = (f32[2,3,640]{2,0,1:T(2,128)S(1)}, f32[2,3,640]{2,0,1:T(2,128)}, u32[]{:S(2)}) copy-start(f32[2,3,640]{2,0,1:T(2,128)} %param.19) | copy-start | bytes 46084
  13.5 50.1 %copy-start.8 = (s32[256,2]{0,1:T(2,128)S(1)}, s32[256,2]{0,1:T(2,128)}, u32[]{:S(2)}) copy-start(s32[256,2]{0,1:T(2,128)} %param.17) | copy-start | bytes 6148
  13.5 50.4 %copy-start.7 = (f32[2,640]{1,0:T(2,128)S(1)}, f32[2,640]{1,0:T(2,128)}, u32[]{:S(2)}) copy-start(f32[2,640]{1,0:T(2,128)} %param.20) | copy-start | bytes 15364
  13.5 42.6 %all-to-all-start.1 = ((bf16[4,64,1,640]{3,0,2,1:T(4,128)(2,1)}), bf16[4,64,1,640]{3,0,2,1:T(4,128)(2,1)S(1)}, u32[]{:S(2)}, u32[]{:S(2)}) async-start(bf16[4,64,1,640]{3,0,2,1:T(4,128)(2,1)} %copy.32), calls=%async_computation.1 | async-start | bytes 655360 | tf_op jit(solution)/shard_map/all_to_all | solution.py:55
  32.4 59.8 %copy-start.9 = (s32[256]{0:T(256)S(1)}, s32[256]{0:T(256)}, u32[]{:S(2)}) copy-start(s32[256]{0:T(256)} %param.18) | copy-start | bytes 3076
  56.1 29.5 %all-to-all-start.2 = ((bf16[4,64,1,640]{3,0,2,1:T(4,128)(2,1)}), bf16[4,64,1,640]{3,0,2,1:T(4,128)(2,1)S(1)}, u32[]{:S(2)}, u32[]{:S(2)}) async-start(bf16[4,64,1,640]{3,0,2,1:T(4,128)(2,1)} %copy.34), calls=%async_computation.2 | async-start | bytes 655360 | tf_op jit(solution)/shard_map/all_to_all | solution.py:56
  85.6 28.9 %all-to-all-start = ((bf16[4,64,1,640]{3,0,2,1:T(4,128)(2,1)}), bf16[4,64,1,640]{3,0,2,1:T(4,128)(2,1)S(1)}, u32[]{:S(2)}, u32[]{:S(2)}) async-start(bf16[4,64,1,640]{3,0,2,1:T(4,128)(2,1)} %copy.31), calls=%async_computation | async-start | bytes 655360 | tf_op jit(solution)/shard_map/all_to_all | solution.py:57
  92.1 205.6 %all-reduce.15.cloned.1.call-start = ((), (), s32[]{:S(2)}) async-start(), calls=%async_computation.6 | async-start | bytes 1310720 | tf_op jit(solution)/shard_map/psum | solution.py:106
  217.2 10.9 %copy-start.3 = (bf16[2,640,320]{1,2,0:T(8,128)(2,1)S(1)}, bf16[2,640,320]{1,2,0:T(8,128)(2,1)}, u32[]{:S(2)}) copy-start(bf16[2,640,320]{1,2,0:T(8,128)(2,1)} %param.21) | copy-start | bytes 2457604
  228.1 1.3 copy-start.4
  230.7 347.1 %all-reduce.9.cloned.1.call-start = ((), (), s32[]{:S(2)}) async-start(), calls=%async_computation.3 | async-start | bytes 2621440
  300.6 460.8 %all-reduce.13.cloned.1.call-start = ((), (), s32[]{:S(2)}) async-start(), calls=%async_computation.5 | async-start | bytes 1310720 | tf_op jit(solution)/shard_map/psum | solution.py:106
  689.2 1.3 copy-start.5
  690.5 71.0 %copy-start.10 = (bf16[2,320,640]{2,1,0:T(8,128)(2,1)S(1)}, bf16[2,320,640]{2,1,0:T(8,128)(2,1)}, u32[]{:S(2)}) copy-start(bf16[2,320,640]{2,1,0:T(8,128)(2,1)} %param.23) | copy-start | bytes 2457604
  691.7 349.7 %all-reduce.11.cloned.1.call-start = ((), (), s32[]{:S(2)}) async-start(), calls=%async_computation.4 | async-start | bytes 2621440
Sparse Core Ops, SparseCore 0:
  230.8 66.8 all-reduce.14
  301.1 276.7 all-reduce.8
  691.8 69.5 all-reduce.12
  764.6 276.7 all-reduce.10
where the time goes:
time: 1050 us
  waiting for transfers between devices  754 us (72%)
  blocking collectives  219 us (21%)
  starting transfers between devices  32.1 us (3%)
  matrix products  14.3 us (1%)
  between operations  14.1 us (1%)
  local copies, waits for them, and re-layouts  10.9 us (1%)
    unnamed x6, waiting for transfers between devices  552 us
    all_gather x2, blocking collectives, per_device(): nodes = lax.all_gather(own_rows, 'gx', axis=0, tiled=True)  199 us
    psum x2, waiting for transfers between devices, per_device(): lax.psum(up_part.astype(jnp.bfloat16), 'ta').astype(jnp.float32)  137 us
    all_to_all x1, waiting for transfers between devices, per_device(): lax.all_to_all(sorted_queries, 'gx', split_axis=1, concat_axis=0, tiled=T...  22.7 us
    all_to_all x1, waiting for transfers between devices, per_device(): lax.all_to_all(sorted_keys, 'gx', split_axis=1, concat_axis=0, tiled=True)  21.6 us
  transfers between devices with their start and end apart: 7, of which 7 were waited for; matrix products, arithmetic and copies ran while one was open for 0% of the time, Pallas kernels for 0%

commit v1 on v0

--- a/solution.py
+++ b/solution.py
@@ -1,3 +1,4 @@
+import functools
 import jax
 import jax.numpy as jnp
 from jax import lax
@@ -10,6 +11,14 @@
 NODE_STEPS = 8
 ROUNDS = 2
 ETYPES = 3
+
+
+def read_region_now(s0, device_axis):
+    mat_out = lax.all_gather(s0, device_axis).sum(axis=0)
+    return mat_out
+
+
+_lift_loops = functools.partial(read_region_now, device_axis="ta")
 
 
 def settle_rows(nodes, hidden, down_local, row_begin, rows_dev):
@@ -103,7 +112,7 @@
         up_part = jnp.dot(normed, up_proj[layer_idx], preferred_element_type=jnp.float32)
         gate_sum, up_sum = (
             lax.psum(gate_part.astype(jnp.bfloat16), "ta").astype(jnp.float32),
-            lax.psum(up_part.astype(jnp.bfloat16), "ta").astype(jnp.float32),
+            _lift_loops(up_part.astype(jnp.bfloat16)).astype(jnp.float32),
         )
         hidden = (jax.nn.silu(gate_sum) * up_sum).astype(jnp.bfloat16)
         down_local = down_proj[layer_idx]

time: 1050 us -> 1120 us (1.067)
  waiting for transfers between devices: 754 us -> 811 us
    all_gather x0 -> x2, waiting for transfers between devices: none -> 48.4 us  [read_region_now(): mat_out = lax.all_gather(s0, device_axis).sum(axis=0)]
    unnamed x6 -> x8, waiting for transfers between devices: 552 us -> 553 us
  transfers between devices with their start and end apart: 7 -> 9, of which waited for: 7 -> 9; matrix products, arithmetic and copies ran while one was open for 0% -> 2% of each run, Pallas kernels for 0% -> 0%
where the time goes in v1:
time: 1120 us
  waiting for transfers between devices  811 us (72%)
  blocking collectives  219 us (20%)
  starting transfers between devices  32.4 us (3%)
  local copies, waits for them, and re-layouts  16.7 us (1%)
  matrix products  16 us (1%)
  between operations  14.5 us (1%)
    unnamed x8, waiting for transfers between devices  553 us
    all_gather x2, blocking collectives, per_device(): nodes = lax.all_gather(own_rows, 'gx', axis=0, tiled=True)  199 us
    psum x2, waiting for transfers between devices, per_device(): lax.psum(gate_part.astype(jnp.bfloat16), 'ta').astype(jnp.float32)  145 us
    all_gather x2, waiting for transfers between devices, read_region_now(): mat_out = lax.all_gather(s0, device_axis).sum(axis=0)  48.4 us
    all_to_all x1, waiting for transfers between devices, per_device(): lax.all_to_all(sorted_queries, 'gx', split_axis=1, concat_axis=0, tiled=T...  22.7 us
  transfers between devices with their start and end apart: 9, of which 9 were waited for; matrix products, arithmetic and copies ran while one was open for 2% of the time, Pallas kernels for 0%

profile of v1, /device:TPU:2, one launch (start us, length us, event | category | flops | bytes accessed | tf_op | source)
XLA Modules:
  0.0 1118.1 jit_solution(7926662437978932111)
XLA Ops:
  6.5 0.7 compare_and_fusion
  7.3 0.2 copy-done
  7.5 1.6 gather_fusion
  9.1 1.6 gather_fusion.1
  10.8 1.6 gather_fusion.2
  12.5 1.0 copy.32
  13.5 18.9 %all-to-all-start.1 = ((bf16[4,64,1,640]{3,0,2,1:T(4,128)(2,1)}), bf16[4,64,1,640]{3,0,2,1:T(4,128)(2,1)S(1)}, u32[]{:S(2)}, u32[]{:S(2)}) async-start(bf16[4,64,1,640]{3,0,2,1:T(4,128)(2,1)} %copy.32), calls=%async_computation.1 | async-start | bytes 655360 | tf_op jit(solution)/shard_map/all_to_all | solution.py:64
  32.4 1.0 copy.34
  33.4 22.7 %all-to-all-done.1 = bf16[4,64,1,640]{3,0,2,1:T(4,128)(2,1)S(1)} async-done(((bf16[4,64,1,640]{3,0,2,1:T(4,128)(2,1)}), bf16[4,64,1,640]{3,0,2,1:T(4,128)(2,1)S(1)}, u32[]{:S(2)}, u32[]{:S(2)}) %all-to-all-start.1) | async-done | bytes 327712 | tf_op jit(solution)/shard_map/all_to_all | solution.py:64
  56.1 6.5 all-to-all-start.2
  62.6 1.0 copy.31
  64.0 21.6 %all-to-all-done.2 = bf16[4,64,1,640]{3,0,2,1:T(4,128)(2,1)S(1)} async-done(((bf16[4,64,1,640]{3,0,2,1:T(4,128)(2,1)}), bf16[4,64,1,640]{3,0,2,1:T(4,128)(2,1)S(1)}, u32[]{:S(2)}, u32[]{:S(2)}) %all-to-all-start.2) | async-done | bytes 327712 | tf_op jit(solution)/shard_map/all_to_all | solution.py:65
  85.6 6.6 all-to-all-start
  92.9 0.5 fusion.68
  93.3 0.3 fusion.5
  93.6 20.9 %all-to-all-done = bf16[4,64,1,640]{3,0,2,1:T(4,128)(2,1)S(1)} async-done(((bf16[4,64,1,640]{3,0,2,1:T(4,128)(2,1)}), bf16[4,64,1,640]{3,0,2,1:T(4,128)(2,1)S(1)}, u32[]{:S(2)}, u32[]{:S(2)}) %all-to-all-start) | async-done | bytes 327712 | tf_op jit(solution)/shard_map/all_to_all | solution.py:66
  114.6 1.4 convolution_bitcast_fusion
  116.0 0.2 copy.37
  116.4 99.8 %all_gather.18 = bf16[512,640]{1,0:T(8,128)(2,1)S(1)} all-gather(bf16[8,640]{1,0:T(8,128)(2,1)S(1)} %multiply_convert_fusion.2), channel_id=1, replica_groups=mesh['gx'=64,'ta'=8] {'gx'}, dimensions={0}, use_global_device_ids=true | all-gather | bytes 665600 | tf_op jit(solution)/shard_map/all_gather | solution.py:89
  216.2 0.3 reshape.148
  216.5 0.7 multiply_reduce_fusion.1
  217.2 0.9 multiply_reduce_fusion.3
  218.1 10.0 psum.28
  228.1 1.3 convolution_convert_fusion.2
  229.5 2.3 convolution_convert_fusion.3
  231.8 22.9 %all-gather.5.cloned.1.call-done = bf16[4096,320]{0,1:T(8,128)(2,1)} async-done(((bf16[512,320]{0,1:T(8,128)(2,1)}), bf16[4096,320]{0,1:T(8,128)(2,1)}) %all-gather.5.cloned.1.call-update) | async-done | bytes 2621456 | tf_op jit(solution)/shard_map/all_gather | solution.py:17
  254.8 2.9 copy.47
  257.7 1.9 bitcast_reduce_fusion.1
  259.6 72.4 %all-reduce.7.cloned.1.call-done = bf16[512,320]{0,1:T(8,128)(2,1)} async-done(((bf16[512,320]{0,1:T(8,128)(2,1)}), bf16[512,320]{0,1:T(8,128)(2,1)}) %all-reduce.7.cloned.1.call-update) | async-done | bytes 327696 | tf_op jit(solution)/shard_map/psum | solution.py:114
  332.0 2.7 fusion.23
  334.8 1.3 dynamic-slice
  336.7 275.6 %all-reduce.11.cloned.1.call-done = f32[512,640]{1,0:T(8,128)} async-done(((f32[512,640]{1,0:T(8,128)}), f32[512,640]{1,0:T(8,128)}) %all-reduce.11.cloned.1.call-update) | async-done | bytes 1310736
  612.3 0.7 fusion.51
  613.1 98.7 %all_gather.21 = bf16[512,640]{1,0:T(8,128)(2,1)S(1)} all-gather(bf16[8,640]{1,0:T(8,128)(2,1)S(1)} %fusion.51), channel_id=1, replica_groups=mesh['gx'=64,'ta'=8] {'gx'}, dimensions={0}, use_global_device_ids=true | all-gather | bytes 665600 | tf_op jit(solution)/shard_map/all_gather | solution.py:123
  711.8 0.3 reshape.149
  712.1 0.7 multiply_reduce_fusion
  712.7 0.9 multiply_reduce_fusion.2
  713.6 10.0 psum.30
  723.7 1.3 convolution_convert_fusion
  725.0 2.3 convolution_convert_fusion.1
  727.3 0.3 all-reduce.13.cloned.1.call-start
  727.6 25.4 %all-gather.7.cloned.1.call-done = bf16[4096,320]{0,1:T(8,128)(2,1)} async-done(((bf16[512,320]{0,1:T(8,128)(2,1)}), bf16[4096,320]{0,1:T(8,128)(2,1)}) %all-gather.7.cloned.1.call-update) | async-done | bytes 2621456 | tf_op jit(solution)/shard_map/all_gather | solution.py:17
  753.0 2.9 copy.48
  755.9 1.9 bitcast_reduce_fusion
  757.9 72.3 %all-reduce.9.cloned.1.call-done = bf16[512,320]{0,1:T(8,128)(2,1)} async-done(((bf16[512,320]{0,1:T(8,128)(2,1)}), bf16[512,320]{0,1:T(8,128)(2,1)}) %all-reduce.9.cloned.1.call-update) | async-done | bytes 327696 | tf_op jit(solution)/shard_map/psum | solution.py:114
  830.2 2.7 fusion.19
  832.9 277.1 %all-reduce.13.cloned.1.call-done = f32[512,640]{1,0:T(8,128)} async-done(((f32[512,640]{1,0:T(8,128)}), f32[512,640]{1,0:T(8,128)}) %all-reduce.13.cloned.1.call-update) | async-done | bytes 1310736
  1110.0 1.3 fusion.50
  (56 shorter events, 1.8 us)
Async XLA Ops:
  6.5 1.0 copy-start
  7.5 1.6 copy-start.1
  9.1 1.6 copy-start.2
  13.5 50.0 %copy-start.4 = (f32[2,3,640]{2,0,1:T(2,128)S(1)}, f32[2,3,640]{2,0,1:T(2,128)}, u32[]{:S(2)}) copy-start(f32[2,3,640]{2,0,1:T(2,128)} %param.19) | copy-start | bytes 46084
  13.5 50.1 %copy-start.6 = (s32[256,2]{0,1:T(2,128)S(1)}, s32[256,2]{0,1:T(2,128)}, u32[]{:S(2)}) copy-start(s32[256,2]{0,1:T(2,128)} %param.17) | copy-start | bytes 6148
  13.5 50.4 %copy-start.5 = (f32[2,640]{1,0:T(2,128)S(1)}, f32[2,640]{1,0:T(2,128)}, u32[]{:S(2)}) copy-start(f32[2,640]{1,0:T(2,128)} %param.20) | copy-start | bytes 15364
  13.5 42.6 %all-to-all-start.1 = ((bf16[4,64,1,640]{3,0,2,1:T(4,128)(2,1)}), bf16[4,64,1,640]{3,0,2,1:T(4,128)(2,1)S(1)}, u32[]{:S(2)}, u32[]{:S(2)}) async-start(bf16[4,64,1,640]{3,0,2,1:T(4,128)(2,1)} %copy.32), calls=%async_computation.1 | async-start | bytes 655360 | tf_op jit(solution)/shard_map/all_to_all | solution.py:64
  32.4 59.8 %copy-start.7 = (s32[256]{0:T(256)S(1)}, s32[256]{0:T(256)}, u32[]{:S(2)}) copy-start(s32[256]{0:T(256)} %param.18) | copy-start | bytes 3076
  56.1 29.5 %all-to-all-start.2 = ((bf16[4,64,1,640]{3,0,2,1:T(4,128)(2,1)}), bf16[4,64,1,640]{3,0,2,1:T(4,128)(2,1)S(1)}, u32[]{:S(2)}, u32[]{:S(2)}) async-start(bf16[4,64,1,640]{3,0,2,1:T(4,128)(2,1)} %copy.34), calls=%async_computation.2 | async-start | bytes 655360 | tf_op jit(solution)/shard_map/all_to_all | solution.py:65
  85.6 28.9 %all-to-all-start = ((bf16[4,64,1,640]{3,0,2,1:T(4,128)(2,1)}), bf16[4,64,1,640]{3,0,2,1:T(4,128)(2,1)S(1)}, u32[]{:S(2)}, u32[]{:S(2)}) async-start(bf16[4,64,1,640]{3,0,2,1:T(4,128)(2,1)} %copy.31), calls=%async_computation | async-start | bytes 655360 | tf_op jit(solution)/shard_map/all_to_all | solution.py:66
  92.1 162.6 %all-gather.5.cloned.1.call-start = ((), (), s32[]{:S(2)}) async-start(), calls=%async_computation.5 | async-start | bytes 2949120 | tf_op jit(solution)/shard_map/all_gather | solution.py:17
  217.2 10.9 copy-start.3
  229.4 102.6 %all-reduce.7.cloned.1.call-start = ((), (), s32[]{:S(2)}) async-start(), calls=%async_computation.3 | async-start | bytes 655360 | tf_op jit(solution)/shard_map/psum | solution.py:114
  231.8 380.5 %all-reduce.11.cloned.1.call-start = ((), (), s32[]{:S(2)}) async-start(), calls=%async_computation.7 | async-start | bytes 2621440
  257.7 74.3 %copy-start.8 = (bf16[2,320,640]{2,1,0:T(8,128)(2,1)S(1)}, bf16[2,320,640]{2,1,0:T(8,128)(2,1)}, u32[]{:S(2)}) copy-start(bf16[2,320,640]{2,1,0:T(8,128)(2,1)} %param.23) | copy-start | bytes 2457604
  334.7 418.3 %all-gather.7.cloned.1.call-start = ((), (), s32[]{:S(2)}) async-start(), calls=%async_computation.6 | async-start | bytes 2949120 | tf_op jit(solution)/shard_map/all_gather | solution.py:17
  725.0 105.2 %all-reduce.9.cloned.1.call-start = ((), (), s32[]{:S(2)}) async-start(), calls=%async_computation.4 | async-start | bytes 655360 | tf_op jit(solution)/shard_map/psum | solution.py:114
  727.3 382.7 %all-reduce.13.cloned.1.call-start = ((), (), s32[]{:S(2)}) async-start(), calls=%async_computation.8 | async-start | bytes 2621440
  755.9 74.3 %copy-start.9 = (bf16[2,320,640]{2,1,0:T(8,128)(2,1)S(1)}, bf16[2,320,640]{2,1,0:T(8,128)(2,1)}, u32[]{:S(2)}) copy-start(bf16[2,320,640]{2,1,0:T(8,128)(2,1)} %param.23) | copy-start | bytes 2457604
Sparse Core Ops, SparseCore 0:
  229.6 25.1 all-gather.4
  257.1 74.8 all-reduce.6
  335.7 276.5 all-reduce.10
  725.1 27.8 all-gather.6
  755.3 74.8 all-reduce.8
  833.4 276.5 all-reduce.12
